TPU v7x, 32 devices: a whole 2x2x4 slice. The times are simulated.
32 devices in a mesh: tm: 4 (over y, core), height: 4 (over z), width: 2 (over x).
Axes of the slice: x: 2, y: 2, z: 4, core: 2. Of those that a mesh axis runs over, the one named last changes fastest.
Arguments:
- tokens: bfloat16 [2048, 3072], P(('tm', 'height', 'width'))
- shift_mod: float32 [3072], replicated, may hold values from -3 to 3
- scale_mod: float32 [3072], replicated, may hold values from -2.5 to 2.5
- proj_weight: bfloat16 [64, 3072], replicated, may hold values from -0.109375 to 0.109375
- proj_bias: float32 [64], replicated, may hold values from -3 to 3
- conv1_weight: bfloat16 [3, 3, 3, 16, 512], replicated, may hold values from -0.3125 to 0.3125
- conv1_bias: float32 [512], replicated, may hold values from -3 to 3
- norm_gain: float32 [512], replicated, may hold values from 0.25 to 1.75
- norm_bias: float32 [512], replicated, may hold values from -3 to 3
- conv2_weight: bfloat16 [3, 3, 3, 512, 512], P(None, None, None, 'width'), may hold values from -0.0546875 to 0.0546875
- conv2_bias: float32 [512], replicated, may hold values from -3 to 3
Outputs:
- pixels: bfloat16 [16, 32, 16, 512], P('tm', 'height', 'width')
All inputs are finite; a program needn't handle non-finite values.
Results may differ from a plain program's by a relative error of at most 0.0095.
Values may be sent and summed in bfloat16 or wider, within the bound.
No kernel may reach another device: no remote copies, remote signals or barrier semaphores. Data moves between devices by JAX's collectives and lax.ppermute only.
A program may use at most 128 MiB of HBM per device.

v0:
```python
import jax
import jax.numpy as jnp
from jax import lax
from jax.sharding import PartitionSpec as P

LAT = 16
C1 = 512
GROUPS = 32
FT = 4
TH = 8
TW = 8
PF = 64


def with_halo(x, sides, width):
    for axis, dim in sides:
        peers, length = (lax.axis_size(axis), x.shape[dim])
        up = [(i, (i + 1) % peers) for i in range(peers - 1)]
        down = [(j, i) for i, j in up]
        last = lax.slice_in_dim(x, length - width, length, axis=dim)
        leading = lax.slice_in_dim(x, 0, width, axis=dim)
        before = lax.ppermute(last, axis, up)
        after = lax.ppermute(leading, axis, down)
        x = jnp.concatenate([before, x, after], axis=dim)
    return x


def shifted(value, axis, steps):
    count = lax.axis_size(axis)
    leading, last = (max(0, -steps), min(count, count - steps))
    return lax.ppermute(value, axis, [(source, source + steps) for source in range(leading, last)])


def project(values_in, shift_mod, scale_mod, proj_weight, proj_bias):
    values = values_in.astype(jnp.float32)
    center = jnp.mean(values, axis=-1, keepdims=True)
    spread = jnp.mean((values - center) * (values - center), axis=-1, keepdims=True)
    normed = ((values - center) * lax.rsqrt(spread + 1e-06) * (1.0 + scale_mod) + shift_mod).astype(
        jnp.bfloat16
    )
    projected = lax.dot_general(
        normed, proj_weight, (((1,), (1,)), ((), ())), preferred_element_type=jnp.float32
    )
    result = (projected + proj_bias).astype(jnp.bfloat16)
    return result


def convolve(padded, weight, frames, rows, cols):
    channels = weight.shape[3]
    outputs = weight.shape[4]
    total = jnp.zeros((frames * rows * cols, outputs), jnp.float32)
    for row_tap in range(3):
        for col_tap in range(3):
            window = jnp.concatenate(
                [
                    padded[
                        frame_tap : frame_tap + frames,
                        row_tap : row_tap + rows,
                        col_tap : col_tap + cols,
                        :,
                    ]
                    for frame_tap in range(3)
                ],
                axis=-1,
            )
            taps = weight[:, row_tap, col_tap].reshape(3 * channels, outputs)
            total = total + jnp.dot(
                window.reshape(-1, 3 * channels), taps, preferred_element_type=jnp.float32
            )
    return total.reshape(frames, rows, cols, outputs)


def per_device(
    tokens,
    shift_mod,
    scale_mod,
    proj_weight,
    proj_bias,
    conv1_weight,
    conv1_bias,
    norm_gain,
    norm_bias,
    conv2_weight,
    conv2_bias,
):
    width_count = lax.axis_size("width")
    height_count = lax.axis_size("height")
    time_count = lax.axis_size("tm")
    line_rows = FT * TH // (2 * width_count)
    half_rows = TH // 2
    half_cols = TW // 2
    local_patches = project(tokens, shift_mod, scale_mod, proj_weight, proj_bias)
    sectioned = local_patches.reshape(line_rows, width_count, half_cols, PF)
    sectioned = lax.all_to_all(sectioned, "width", split_axis=1, concat_axis=0, tiled=True)
    sectioned = sectioned.reshape(FT // height_count, height_count, half_rows, half_cols, PF)
    sectioned = lax.all_to_all(sectioned, "height", split_axis=1, concat_axis=0, tiled=True)
    patches = sectioned.reshape(FT, half_rows, half_cols, PF)
    latent = (
        patches.reshape(FT, half_rows, half_cols, LAT, 2, 2)
        .transpose(0, 1, 4, 2, 5, 3)
        .reshape(FT, TH, TW, LAT)
    )
    group_size = C1 // GROUPS
    count = FT * TH * TW * time_count * height_count * width_count * group_size
    padded = with_halo(latent, (("height", 1), ("width", 2)), 2)
    earlier = shifted(padded, "tm", 1)
    stacked = jnp.concatenate([earlier, padded], axis=0)
    hidden = (convolve(stacked, conv1_weight, FT + 2, TH + 2, TW + 2) + conv1_bias).astype(
        jnp.bfloat16
    )
    grouped = hidden[2:, 1:-1, 1:-1].astype(jnp.float32).reshape(-1, GROUPS, group_size)
    sums = jnp.sum(grouped, axis=(0, 2))
    squares = jnp.sum(grouped * grouped, axis=(0, 2))
    sums, squares = lax.psum((sums, squares), ("tm", "height", "width"))
    gmean = sums / count
    gvar = squares / count - gmean * gmean
    mean_full = jnp.repeat(gmean, group_size)
    inverse_full = jnp.repeat(lax.rsqrt(gvar + 1e-06), group_size)
    scaled = (hidden.astype(jnp.float32) - mean_full) * inverse_full * norm_gain + norm_bias
    activated = jax.nn.silu(scaled).astype(jnp.bfloat16)
    frame_global = lax.axis_index("tm") * FT - 2 + jnp.arange(FT + 2)
    row_global = lax.axis_index("height") * TH - 1 + jnp.arange(TH + 2)
    col_global = lax.axis_index("width") * TW - 1 + jnp.arange(TW + 2)
    frame_valid = frame_global >= 0
    row_valid = (row_global >= 0) & (row_global < TH * height_count)
    col_valid = (col_global >= 0) & (col_global < TW * width_count)
    inside = (
        frame_valid[:, None, None, None]
        & row_valid[None, :, None, None]
        & col_valid[None, None, :, None]
    )
    act_stacked = jnp.where(inside, activated, jnp.zeros_like(activated))
    total = convolve(
        act_stacked, lax.all_gather(conv2_weight, "width", axis=3, tiled=True), FT, TH, TW
    )
    return (total + conv2_bias).astype(jnp.bfloat16)


def solution(mesh):
    placed = (
        P(("tm", "height", "width"), None),
        P(),
        P(),
        P(),
        P(),
        P(),
        P(),
        P(),
        P(),
        P(None, None, None, "width", None),
        P(),
    )
    return jax.shard_map(
        per_device,
        mesh=mesh,
        in_specs=placed,
        out_specs=P("tm", "height", "width", None),
        check_vma=False,
    )
```

profile of v0, /device:TPU:0, one launch (start us, length us, event | category | flops | bytes accessed | tf_op | source)
XLA Modules:
  0.0 205.0 jit_solution(6254833569561330727)
XLA Ops:
  6.6 0.7 all-gather.2.cloned.1.call-update
  8.5 0.7 reshape.178
  9.1 4.2 %all-to-all-start = ((bf16[2,2,1024]{2,1,0:T(2,128)(2,1)}), bf16[2,2,1024]{2,1,0:T(2,128)(2,1)S(1)}, u32[]{:S(2)}, u32[]{:S(2)}) async-start(bf16[2,2,1024]{2,1,0:T(2,128)(2,1)} %reshape.178), calls=%async_computation | async-start | bytes 16384 | tf_op jit(solution)/shard_map/all_to_all | solution.py:94
  13.4 0.8 fusion.17
  14.1 3.1 %all-to-all-done = bf16[2,2,1024]{2,1,0:T(2,128)(2,1)S(1)} async-done(((bf16[2,2,1024]{2,1,0:T(2,128)(2,1)}), bf16[2,2,1024]{2,1,0:T(2,128)(2,1)S(1)}, u32[]{:S(2)}, u32[]{:S(2)}) %all-to-all-start) | async-done | bytes 8224 | tf_op jit(solution)/shard_map/all_to_all | solution.py:94
  17.3 0.7 reshape.180
  18.0 5.3 %all-to-all-start.1 = ((bf16[4,2,512]{2,1,0:T(2,128)(2,1)}), bf16[4,2,512]{2,1,0:T(2,128)(2,1)S(1)}, u32[]{:S(2)}, u32[]{:S(2)}) async-start(bf16[4,2,512]{2,1,0:T(2,128)(2,1)} %reshape.180), calls=%async_computation.1 | async-start | bytes 16384 | tf_op jit(solution)/shard_map/all_to_all | solution.py:96
  23.3 5.6 %all-to-all-done.1 = bf16[4,2,512]{2,1,0:T(2,128)(2,1)S(1)} async-done(((bf16[4,2,512]{2,1,0:T(2,128)(2,1)}), bf16[4,2,512]{2,1,0:T(2,128)(2,1)S(1)}, u32[]{:S(2)}, u32[]{:S(2)}) %all-to-all-start.1) | async-done | bytes 8224 | tf_op jit(solution)/shard_map/all_to_all | solution.py:96
  29.7 2.5 %collective-permute-start = (bf16[4,2,8,16]{3,2,1,0:T(8,128)(2,1)S(1)}, bf16[4,2,8,16]{3,2,1,0:T(8,128)(2,1)S(1)}, u32[]{:S(2)}, u32[]{:S(2)}) collective-permute-start(bf16[4,2,8,16]{3,2,1,0:T(8,128)(2,1)S(1)} %get-tuple-element.83), channel_id=1, source_target_pairs={{0,2},{2,4},{4,6},{1,3},{3,5},{5,7},{8,10},{10,12},{12,14},{9,11},... | collective-permute-start | bytes 6152 | tf_op jit(solution)/shard_map/ppermute | solution.py:22
  32.2 1.3 collective-permute-start.1
  33.7 4.2 %collective-permute-done.1 = bf16[4,2,8,16]{3,2,1,0:T(8,128)(2,1)S(1)} collective-permute-done((bf16[4,2,8,16]{3,2,1,0:T(8,128)(2,1)S(1)}, bf16[4,2,8,16]{3,2,1,0:T(8,128)(2,1)S(1)}, u32[]{:S(2)}, u32[]{:S(2)}) %collective-permute-start.1) | collective-permute-done | bytes 2080 | tf_op jit(solution)/shard_map/ppermute | solution.py:23
  37.9 1.9 collective-permute-start.2
  39.8 1.3 collective-permute-start.3
  41.2 0.6 collective-permute-done.2
  41.8 4.4 %collective-permute-done.3 = bf16[4,12,2,16]{3,2,1,0:T(2,128)(2,1)S(1)} collective-permute-done((bf16[4,12,2,16]{3,2,1,0:T(2,128)(2,1)S(1)}, bf16[4,12,2,16]{3,2,1,0:T(2,128)(2,1)S(1)}, u32[]{:S(2)}, u32[]{:S(2)}) %collective-permute-start.3) | collective-permute-done | bytes 3104 | tf_op jit(solution)/shard_map/ppermute | solution.py:23
  46.3 1.3 collective-permute-start.4
  47.7 1.0 collective-permute-done.4
  48.8 1.1 fusion.19
  50.4 0.7 reshape.158
  51.1 0.7 reshape.159
  51.9 1.6 fusion.18
  53.8 2.7 %pad_maximum_fusion.11 = (bf16[6,10,10,48]{3,2,1,0:T(8,128)(2,1)}, bf16[6,10,10,48]{3,2,1,0:T(8,128)(2,1)S(1)}) fusion(bf16[6,10,10,16]{3,2,1,0:T(8,128)(2,1)} %get-tuple-element.72, bf16[6,10,10,16]{3,2,1,0:T(8,128)(2,1)} %get-tuple-element.74, bf16[6,10,10,16]{3,2,1,0:T(8,128)(2,1)} %get-tuple-element.73, bf16[6,10,10,16]{3,2,1,0:T(8,128)(2,1)} %get-tuple-element.69, ...), kind=kLoop, calls=%fused_computation.49 | loop fusion | flops 345600 | bytes 230400 | tf_op jit(solution)/shard_map/concatenate | solution.py:54
  56.5 1.7 reshape.160
  58.2 0.8 reshape.161
  58.9 1.2 pad_maximum_fusion.15
  60.1 1.0 reshape.164
  66.4 1.3 convolution_add_fusion
  67.7 1.4 reshape.167
  70.1 43.8 %all-reduce = (f32[32]{0:T(128)S(1)}, f32[32]{0:T(128)S(1)}) all-reduce(f32[32]{0:T(128)S(1)} %reduce_sum.57, f32[32]{0:T(128)S(1)} %reduce_sum.54), channel_id=1, replica_groups=mesh['tm'=4,'height'=4,'width'=2] {'tm','height','width'}, use_global_device_ids=true, to_apply=%region_7.8 | all-reduce | flops 64 | bytes 512 | tf_op jit(solution)/shard_map/psum | solution.py:114
  114.2 0.8 fusion.1
  115.4 0.8 fusion.15
  116.2 1.0 pad_maximum_fusion.2
  117.2 1.0 pad_maximum_fusion.6
  118.2 0.9 pad_maximum_fusion.5
  119.1 1.0 pad_maximum_fusion.4
  120.1 1.0 pad_maximum_fusion.3
  121.1 62.3 %all-gather.2.cloned.1.call-done = bf16[3,3,3,512,512]{4,3,2,1,0:T(8,128)(2,1)} async-done(((bf16[3,3,3,256,512]{4,3,2,1,0:T(8,128)(2,1)}), bf16[3,3,3,512,512]{4,3,2,1,0:T(8,128)(2,1)}) %all-gather.2.cloned.1.call-update) | async-done | bytes 14155792 | tf_op jit(solution)/shard_map/all_gather | solution.py:134
  183.4 5.9 %fusion.14 = (bf16[3,1,1,512,512]{4,3,2,1,0:T(8,128)(2,1)S(1)}, bf16[3,1,1,512,512]{4,3,2,1,0:T(8,128)(2,1)S(1)}, bf16[3,1,1,512,512]{4,3,2,1,0:T(8,128)(2,1)S(1...) fusion(bf16[3,3,3,512,512]{4,3,2,1,0:T(8,128)(2,1)} %all-gather, ...), kind=kLoop, calls=%fused_computation.70 | loop fusion | bytes 28311552 | tf_op jit(solution)/shard_map/slice | solution.py:66
  189.3 0.6 fusion.22
  189.9 0.6 convolution_add_fusion.15
  191.0 0.6 convolution_add_fusion.14
  192.1 0.6 convolution_add_fusion.13
  193.3 0.6 convolution_add_fusion.12
  194.4 0.6 convolution_add_fusion.11
  195.5 0.6 convolution_add_fusion.10
  196.1 0.6 convolution_add_fusion.9
  196.7 0.6 convolution_add_fusion.8
  197.4 0.7 add_convert_fusion.1
  (109 shorter events, 13.1 us)
Async XLA Ops:
  6.5 1.5 copy-start
  6.5 1.0 copy-start.7
  6.5 1.5 copy-start.20
  6.5 1.5 copy-start.26
  6.5 1.5 copy-start.25
  6.5 176.8 %all-gather.2.cloned.1.call-start = ((), (), s32[]{:S(2)}) async-start(), calls=%async_computation.2 | async-start | bytes 21233664 | tf_op jit(solution)/shard_map/all_gather | solution.py:134
  7.6 5.8 %copy-start.12 = (bf16[3,3,3,16,512]{4,3,2,1,0:T(8,128)(2,1)S(1)}, bf16[3,3,3,16,512]{4,3,2,1,0:T(8,128)(2,1)}, u32[]{:S(2)}) copy-start(bf16[3,3,3,16,512]{4,3,2,1,0:T(8,128)(2,1)} %param.16) | copy-start | bytes 1327108
  9.1 8.1 %all-to-all-start = ((bf16[2,2,1024]{2,1,0:T(2,128)(2,1)}), bf16[2,2,1024]{2,1,0:T(2,128)(2,1)S(1)}, u32[]{:S(2)}, u32[]{:S(2)}) async-start(bf16[2,2,1024]{2,1,0:T(2,128)(2,1)} %reshape.178), calls=%async_computation | async-start | bytes 16384 | tf_op jit(solution)/shard_map/all_to_all | solution.py:94
  18.0 10.9 %all-to-all-start.1 = ((bf16[4,2,512]{2,1,0:T(2,128)(2,1)}), bf16[4,2,512]{2,1,0:T(2,128)(2,1)S(1)}, u32[]{:S(2)}, u32[]{:S(2)}) async-start(bf16[4,2,512]{2,1,0:T(2,128)(2,1)} %reshape.180), calls=%async_computation.1 | async-start | bytes 16384 | tf_op jit(solution)/shard_map/all_to_all | solution.py:96
  29.7 4.0 %collective-permute-start = (bf16[4,2,8,16]{3,2,1,0:T(8,128)(2,1)S(1)}, bf16[4,2,8,16]{3,2,1,0:T(8,128)(2,1)S(1)}, u32[]{:S(2)}, u32[]{:S(2)}) collective-permute-start(bf16[4,2,8,16]{3,2,1,0:T(8,128)(2,1)S(1)} %get-tuple-element.83), channel_id=1, source_target_pairs={{0,2},{2,4},{4,6},{1,3},{3,5},{5,7},{8,10},{10,12},{12,14},{9,11},... | collective-permute-start | bytes 6152 | tf_op jit(solution)/shard_map/ppermute | solution.py:22
  32.2 5.6 %collective-permute-start.1 = (bf16[4,2,8,16]{3,2,1,0:T(8,128)(2,1)S(1)}, bf16[4,2,8,16]{3,2,1,0:T(8,128)(2,1)S(1)}, u32[]{:S(2)}, u32[]{:S(2)}) collective-permute-start(bf16[4,2,8,16]{3,2,1,0:T(8,128)(2,1)S(1)} %get-tuple-element.84), channel_id=1, source_target_pairs={{2,0},{4,2},{6,4},{3,1},{5,3},{7,5},{10,8},{12,10},{14,12},{11,9},... | collective-permute-start | bytes 6152 | tf_op jit(solution)/shard_map/ppermute | solution.py:23
  37.9 3.9 %collective-permute-start.2 = (bf16[4,12,2,16]{3,2,1,0:T(2,128)(2,1)S(1)}, bf16[4,12,2,16]{3,2,1,0:T(2,128)(2,1)S(1)}, u32[]{:S(2)}, u32[]{:S(2)}) collective-permute-start(bf16[4,12,2,16]{3,2,1,0:T(2,128)(2,1)S(1)} %get-tuple-element.81), channel_id=1, source_target_pairs={{0,1},{2,3},{4,5},{6,7},{8,9},{10,11},{12,13},{14,15},{16,17},{18,... | collective-permute-start | bytes 9224 | tf_op jit(solution)/shard_map/ppermute | solution.py:22
  39.8 6.4 %collective-permute-start.3 = (bf16[4,12,2,16]{3,2,1,0:T(2,128)(2,1)S(1)}, bf16[4,12,2,16]{3,2,1,0:T(2,128)(2,1)S(1)}, u32[]{:S(2)}, u32[]{:S(2)}) collective-permute-start(bf16[4,12,2,16]{3,2,1,0:T(2,128)(2,1)S(1)} %get-tuple-element.82), channel_id=1, source_target_pairs={{1,0},{3,2},{5,4},{7,6},{9,8},{11,10},{13,12},{15,14},{17,16},{19,... | collective-permute-start | bytes 9224 | tf_op jit(solution)/shard_map/ppermute | solution.py:23
  46.3 2.4 %collective-permute-start.4 = (bf16[4,12,12,16]{3,2,1,0:T(8,128)(2,1)S(1)}, bf16[4,12,12,16]{3,2,1,0:T(8,128)(2,1)S(1)}, u32[]{:S(2)}, u32[]{:S(2)}) collective-permute-start(bf16[4,12,12,16]{3,2,1,0:T(8,128)(2,1)S(1)} %pad_maximum_fusion.18), channel_id=1, source_target_pairs={{0,8},{8,16},{16,24},{1,9},{9,17},{17,25},{2,10},{10,18},{18,26},{... | collective-permute-start | bytes 55304 | tf_op jit(solution)/shard_map/ppermute | solution.py:31
  61.1 0.9 copy-start.8
  61.7 0.9 copy-start.9
  61.7 0.9 copy-start.19
  62.3 0.9 copy-start.11
  62.3 0.9 copy-start.18
  63.0 0.9 copy-start.10
  63.0 0.9 copy-start.17
  63.6 0.8 copy-start.16
  64.2 0.8 copy-start.15
  64.7 0.8 copy-start.14
  65.3 0.8 copy-start.13
  67.7 1.4 copy-start.21
  69.1 45.1 %copy-start.22 = (f32[512]{0:T(512)S(1)}, f32[512]{0:T(512)}, u32[]{:S(2)}) copy-start(f32[512]{0:T(512)} %param.19) | copy-start | bytes 6148
  69.1 45.1 %copy-start.23 = (f32[512]{0:T(512)S(1)}, f32[512]{0:T(512)}, u32[]{:S(2)}) copy-start(f32[512]{0:T(512)} %param.18) | copy-start | bytes 6148
  189.9 1.1 copy-start.3
  191.0 1.1 copy-start.6
  192.1 1.1 copy-start.5
  193.3 1.1 copy-start.4
  194.4 1.1 copy-start.2
  196.7 1.5 copy-start.1
  196.7 0.7 copy-start.24
Sparse Core Ops, SparseCore 0:
  8.9 174.3 all-gather.1
where the time goes:
time: 206 us; the launch traced here: 205 us
  waiting for transfers between devices  82 us (40%)
  blocking collectives  43.8 us (21%)
  local copies, waits for them, and re-layouts  25 us (12%)
  starting transfers between devices  17.9 us (9%)
  between operations  14 us (7%)
  other arithmetic  13.3 us (6%)
  matrix products  9.1 us (4%)
    all_gather x1, waiting for transfers between devices, per_device(): lax.all_gather(conv2_weight, 'width', axis=3, tiled=True)  62.3 us
    psum x1, blocking collectives, per_device(): sums, squares = lax.psum((sums, squares), ('tm', 'height', 'width'))  43.8 us
    concatenate x14, other arithmetic, convolve(): jnp.concatenate([padded[frame_tap:frame_tap + frames, row_tap:row_tap + r...  10.1 us
    dot_general x18, matrix products, convolve(): jnp.dot(window.reshape(-1, 3 * channels), taps, preferred_element_type=jn...  8.74 us
    ppermute x2, waiting for transfers between devices, with_halo(): after = lax.ppermute(leading, axis, down)  8.6 us
    unnamed x58, local copies, waits for them, and re-layouts  6.88 us
    slice x2, local copies, waits for them, and re-layouts, convolve(): taps = weight[:, row_tap, col_tap].reshape(3 * channels, outputs)  6.68 us
    all_to_all x1, waiting for transfers between devices, per_device(): lax.all_to_all(sectioned, 'height', split_axis=1, concat_axis=0, tiled=True)  5.58 us
  transfers between devices with their start and end apart: 8, of which 8 were waited for; matrix products, arithmetic and copies ran while one was open for 15% of the time, Pallas kernels for 0%

commit v1 on v0

--- a/solution.py
+++ b/solution.py
@@ -10,6 +10,12 @@
 TH = 8
 TW = 8
 PF = 64
+
+
+def gathered_along(x, mesh_axis, along):
+    shards = lax.all_gather(x, mesh_axis, axis=0, tiled=False)
+    whole = jnp.concatenate(shards, axis=along)
+    return whole
 
 
 def with_halo(x, sides, width):
@@ -130,9 +136,7 @@
         & col_valid[None, None, :, None]
     )
     act_stacked = jnp.where(inside, activated, jnp.zeros_like(activated))
-    total = convolve(
-        act_stacked, lax.all_gather(conv2_weight, "width", axis=3, tiled=True), FT, TH, TW
-    )
+    total = convolve(act_stacked, gathered_along(conv2_weight, "width", 3), FT, TH, TW)
     return (total + conv2_bias).astype(jnp.bfloat16)
 
 

time: 206 us -> 212 us (1.029)
  local copies, waits for them, and re-layouts: 25 us -> 29.6 us
  waiting for transfers between devices: 82 us -> 78.3 us
  other arithmetic: 13.3 us -> 16.8 us
    reshape x0 -> x1, local copies, waits for them, and re-layouts: none -> 6.78 us  [gathered_along(): whole = jnp.concatenate(shards, axis=along)]
    all_gather x1, waiting for transfers between devices: 62.3 us -> 58.7 us  [gathered_along(): shards = lax.all_gather(x, mesh_axis, axis=0, tiled=False)]
    concatenate x14, other arithmetic: 10.1 us -> 13.6 us  [convolve(): jnp.concatenate([padded[frame_tap:frame_tap + frames, row_tap:row_tap + r...]
    slice x2, local copies, waits for them, and re-layouts: 6.68 us -> 3.32 us  [convolve(): taps = weight[:, row_tap, col_tap].reshape(3 * channels, outputs)]
    unnamed x58 -> x64, local copies, waits for them, and re-layouts: 6.88 us -> 7.95 us
  transfers between devices with their start and end apart: 8 -> 8, of which waited for: 8 -> 8; matrix products, arithmetic and copies ran while one was open for 15% -> 16% of each run, Pallas kernels for 0% -> 0%
where the time goes in v1:
time: 212 us; the launch traced here: 211 us
  waiting for transfers between devices  78.3 us (37%)
  blocking collectives  43.8 us (21%)
  local copies, waits for them, and re-layouts  29.6 us (14%)
  starting transfers between devices  17.9 us (8%)
  other arithmetic  16.8 us (8%)
  between operations  13.9 us (7%)
  matrix products  10.8 us (5%)
    all_gather x1, waiting for transfers between devices, gathered_along(): shards = lax.all_gather(x, mesh_axis, axis=0, tiled=False)  58.7 us
    psum x1, blocking collectives, per_device(): sums, squares = lax.psum((sums, squares), ('tm', 'height', 'width'))  43.8 us
    concatenate x14, other arithmetic, convolve(): jnp.concatenate([padded[frame_tap:frame_tap + frames, row_tap:row_tap + r...  13.6 us
    dot_general x18, matrix products, convolve(): jnp.dot(window.reshape(-1, 3 * channels), taps, preferred_element_type=jn...  10.5 us
    ppermute x2, waiting for transfers between devices, with_halo(): after = lax.ppermute(leading, axis, down)  8.6 us
    unnamed x64, local copies, waits for them, and re-layouts  7.95 us
    reshape x1, local copies, waits for them, and re-layouts, gathered_along(): whole = jnp.concatenate(shards, axis=along)  6.78 us
    all_to_all x1, waiting for transfers between devices, per_device(): lax.all_to_all(sectioned, 'height', split_axis=1, concat_axis=0, tiled=True)  5.58 us
  transfers between devices with their start and end apart: 8, of which 8 were waited for; matrix products, arithmetic and copies ran while one was open for 16% of the time, Pallas kernels for 0%

profile of v1, /device:TPU:0, one launch (start us, length us, event | category | flops | bytes accessed | tf_op | source)
XLA Modules:
  0.0 211.2 jit_solution(11491127193564791336)
XLA Ops:
  6.6 0.7 all-gather.3.cloned.1.call-update
  8.5 0.7 reshape.187
  9.1 4.2 %all-to-all-start = ((bf16[2,2,1024]{2,1,0:T(2,128)(2,1)}), bf16[2,2,1024]{2,1,0:T(2,128)(2,1)S(1)}, u32[]{:S(2)}, u32[]{:S(2)}) async-start(bf16[2,2,1024]{2,1,0:T(2,128)(2,1)} %reshape.187), calls=%async_computation | async-start | bytes 16384 | tf_op jit(solution)/shard_map/all_to_all | solution.py:100
  13.4 0.7 fusion.17
  14.1 3.1 %all-to-all-done = bf16[2,2,1024]{2,1,0:T(2,128)(2,1)S(1)} async-done(((bf16[2,2,1024]{2,1,0:T(2,128)(2,1)}), bf16[2,2,1024]{2,1,0:T(2,128)(2,1)S(1)}, u32[]{:S(2)}, u32[]{:S(2)}) %all-to-all-start) | async-done | bytes 8224 | tf_op jit(solution)/shard_map/all_to_all | solution.py:100
  17.3 0.7 reshape.189
  18.0 5.3 %all-to-all-start.1 = ((bf16[4,2,512]{2,1,0:T(2,128)(2,1)}), bf16[4,2,512]{2,1,0:T(2,128)(2,1)S(1)}, u32[]{:S(2)}, u32[]{:S(2)}) async-start(bf16[4,2,512]{2,1,0:T(2,128)(2,1)} %reshape.189), calls=%async_computation.1 | async-start | bytes 16384 | tf_op jit(solution)/shard_map/all_to_all | solution.py:102
  23.3 5.6 %all-to-all-done.1 = bf16[4,2,512]{2,1,0:T(2,128)(2,1)S(1)} async-done(((bf16[4,2,512]{2,1,0:T(2,128)(2,1)}), bf16[4,2,512]{2,1,0:T(2,128)(2,1)S(1)}, u32[]{:S(2)}, u32[]{:S(2)}) %all-to-all-start.1) | async-done | bytes 8224 | tf_op jit(solution)/shard_map/all_to_all | solution.py:102
  29.7 2.5 %collective-permute-start = (bf16[4,2,8,16]{3,2,1,0:T(8,128)(2,1)S(1)}, bf16[4,2,8,16]{3,2,1,0:T(8,128)(2,1)S(1)}, u32[]{:S(2)}, u32[]{:S(2)}) collective-permute-start(bf16[4,2,8,16]{3,2,1,0:T(8,128)(2,1)S(1)} %get-tuple-element.83), channel_id=1, source_target_pairs={{0,2},{2,4},{4,6},{1,3},{3,5},{5,7},{8,10},{10,12},{12,14},{9,11},... | collective-permute-start | bytes 6152 | tf_op jit(solution)/shard_map/ppermute | solution.py:28
  32.2 1.3 collective-permute-start.1
  33.7 4.2 %collective-permute-done.1 = bf16[4,2,8,16]{3,2,1,0:T(8,128)(2,1)S(1)} collective-permute-done((bf16[4,2,8,16]{3,2,1,0:T(8,128)(2,1)S(1)}, bf16[4,2,8,16]{3,2,1,0:T(8,128)(2,1)S(1)}, u32[]{:S(2)}, u32[]{:S(2)}) %collective-permute-start.1) | collective-permute-done | bytes 2080 | tf_op jit(solution)/shard_map/ppermute | solution.py:29
  37.9 1.9 collective-permute-start.2
  39.8 1.3 collective-permute-start.3
  41.2 0.6 collective-permute-done.2
  41.8 4.4 %collective-permute-done.3 = bf16[4,12,2,16]{3,2,1,0:T(2,128)(2,1)S(1)} collective-permute-done((bf16[4,12,2,16]{3,2,1,0:T(2,128)(2,1)S(1)}, bf16[4,12,2,16]{3,2,1,0:T(2,128)(2,1)S(1)}, u32[]{:S(2)}, u32[]{:S(2)}) %collective-permute-start.3) | collective-permute-done | bytes 3104 | tf_op jit(solution)/shard_map/ppermute | solution.py:29
  46.3 1.3 collective-permute-start.4
  47.7 1.0 collective-permute-done.4
  48.9 1.1 fusion.19
  50.4 0.7 reshape.164
  51.2 0.7 reshape.165
  51.9 1.6 fusion.18
  53.9 2.7 %pad_maximum_fusion.11 = (bf16[6,10,10,48]{3,2,1,0:T(8,128)(2,1)}, bf16[6,10,10,48]{3,2,1,0:T(8,128)(2,1)S(1)}) fusion(bf16[6,10,10,16]{3,2,1,0:T(8,128)(2,1)} %get-tuple-element.72, bf16[6,10,10,16]{3,2,1,0:T(8,128)(2,1)} %get-tuple-element.74, bf16[6,10,10,16]{3,2,1,0:T(8,128)(2,1)} %get-tuple-element.73, bf16[6,10,10,16]{3,2,1,0:T(8,128)(2,1)} %get-tuple-element.69, ...), kind=kLoop, calls=%fused_computation.49 | loop fusion | flops 345600 | bytes 230400 | tf_op jit(solution)/shard_map/concatenate | solution.py:60
  56.5 1.7 reshape.166
  58.2 0.7 reshape.167
  59.0 1.2 pad_maximum_fusion.15
  60.1 1.0 reshape.170
  66.4 1.3 convolution_add_fusion
  67.8 1.4 reshape.173
  70.1 43.8 %all-reduce = (f32[32]{0:T(128)S(1)}, f32[32]{0:T(128)S(1)}) all-reduce(f32[32]{0:T(128)S(1)} %reduce_sum.57, f32[32]{0:T(128)S(1)} %reduce_sum.54), channel_id=1, replica_groups=mesh['tm'=4,'height'=4,'width'=2] {'tm','height','width'}, use_global_device_ids=true, to_apply=%region_7.8 | all-reduce | flops 64 | bytes 512 | tf_op jit(solution)/shard_map/psum | solution.py:120
  114.3 0.8 fusion.1
  115.4 1.0 pad_maximum_fusion.1
  116.3 0.9 pad_maximum_fusion
  117.3 0.8 fusion.15
  118.0 1.0 pad_maximum_fusion.8
  119.0 1.0 pad_maximum_fusion.2
  120.0 0.9 pad_maximum_fusion.7
  120.9 0.9 pad_maximum_fusion.6
  121.9 0.9 pad_maximum_fusion.5
  122.8 1.0 pad_maximum_fusion.4
  123.8 0.9 pad_maximum_fusion.3
  124.7 58.7 %all-gather.3.cloned.1.call-done = bf16[6,3,3,256,512]{4,3,2,1,0:T(8,128)(2,1)} async-done(((bf16[3,3,3,256,512]{4,3,2,1,0:T(8,128)(2,1)}), bf16[6,3,3,256,512]{4,3,2,1,0:T(8,128)(2,1)}) %all-gather.3.cloned.1.call-update) | async-done | bytes 14155792 | tf_op jit(solution)/shard_map/all_gather | solution.py:16
  183.4 6.8 %copy.24 = bf16[3,3,3,2,256,512]{5,4,3,2,1,0:T(8,128)(2,1)S(1)} copy(bf16[3,3,3,2,256,512]{5,4,2,1,0,3:T(8,128)(2,1)} %bitcast.88) | data formatting | bytes 28311552 | tf_op jit(solution)/shard_map/reshape | solution.py:17
  190.1 2.6 %fusion.14 = (bf16[3,1,1,512,512]{4,3,2,1,0:T(8,128)(2,1)S(1)}, bf16[3,1,1,512,512]{4,3,2,1,0:T(8,128)(2,1)S(1)}, bf16[3,1,1,512,512]{4,3,2,1,0:T(8,128)(2,1)S(1...) fusion(bf16[3,3,3,512,512]{4,3,2,1,0:T(8,128)(2,1)S(1)} %bitcast.87), kind=kLoop, calls=%fused_computation.70 | loop fusion | bytes 28311552 | tf_op jit(solution)/shard_map/slice | solution.py:72
  192.7 2.3 %fusion.22 = f32[256,512]{1,0:T(8,128)S(1)} fusion(bf16[256,1536]{1,0:T(8,128)(2,1)} %bitcast.98, bf16[1536,512]{1,0:T(8,128)(2,1)} %bitcast.97), kind=kOutput, calls=%fused_computation.80 | convolution fusion | flops 402653184 | bytes 2883584 | tf_op jit(solution)/shard_map/dot_general | solution.py:73
  195.0 0.6 convolution_add_fusion.15
  196.1 0.6 convolution_add_fusion.14
  198.4 0.6 convolution_add_fusion.12
  203.6 0.7 add_convert_fusion.1
  (116 shorter events, 16.9 us)
Async XLA Ops:
  6.5 1.5 copy-start
  6.5 1.0 copy-start.10
  6.5 1.5 copy-start.23
  6.5 1.5 copy-start.29
  6.5 1.5 copy-start.28
  6.5 176.8 %all-gather.3.cloned.1.call-start = ((), (), s32[]{:S(2)}) async-start(), calls=%async_computation.2 | async-start | bytes 21233664 | tf_op jit(solution)/shard_map/all_gather | solution.py:16
  7.6 5.8 %copy-start.15 = (bf16[3,3,3,16,512]{4,3,2,1,0:T(8,128)(2,1)S(1)}, bf16[3,3,3,16,512]{4,3,2,1,0:T(8,128)(2,1)}, u32[]{:S(2)}) copy-start(bf16[3,3,3,16,512]{4,3,2,1,0:T(8,128)(2,1)} %param.16) | copy-start | bytes 1327108
  9.1 8.1 %all-to-all-start = ((bf16[2,2,1024]{2,1,0:T(2,128)(2,1)}), bf16[2,2,1024]{2,1,0:T(2,128)(2,1)S(1)}, u32[]{:S(2)}, u32[]{:S(2)}) async-start(bf16[2,2,1024]{2,1,0:T(2,128)(2,1)} %reshape.187), calls=%async_computation | async-start | bytes 16384 | tf_op jit(solution)/shard_map/all_to_all | solution.py:100
  18.0 10.9 %all-to-all-start.1 = ((bf16[4,2,512]{2,1,0:T(2,128)(2,1)}), bf16[4,2,512]{2,1,0:T(2,128)(2,1)S(1)}, u32[]{:S(2)}, u32[]{:S(2)}) async-start(bf16[4,2,512]{2,1,0:T(2,128)(2,1)} %reshape.189), calls=%async_computation.1 | async-start | bytes 16384 | tf_op jit(solution)/shard_map/all_to_all | solution.py:102
  29.7 4.0 %collective-permute-start = (bf16[4,2,8,16]{3,2,1,0:T(8,128)(2,1)S(1)}, bf16[4,2,8,16]{3,2,1,0:T(8,128)(2,1)S(1)}, u32[]{:S(2)}, u32[]{:S(2)}) collective-permute-start(bf16[4,2,8,16]{3,2,1,0:T(8,128)(2,1)S(1)} %get-tuple-element.83), channel_id=1, source_target_pairs={{0,2},{2,4},{4,6},{1,3},{3,5},{5,7},{8,10},{10,12},{12,14},{9,11},... | collective-permute-start | bytes 6152 | tf_op jit(solution)/shard_map/ppermute | solution.py:28
  32.2 5.6 %collective-permute-start.1 = (bf16[4,2,8,16]{3,2,1,0:T(8,128)(2,1)S(1)}, bf16[4,2,8,16]{3,2,1,0:T(8,128)(2,1)S(1)}, u32[]{:S(2)}, u32[]{:S(2)}) collective-permute-start(bf16[4,2,8,16]{3,2,1,0:T(8,128)(2,1)S(1)} %get-tuple-element.84), channel_id=1, source_target_pairs={{2,0},{4,2},{6,4},{3,1},{5,3},{7,5},{10,8},{12,10},{14,12},{11,9},... | collective-permute-start | bytes 6152 | tf_op jit(solution)/shard_map/ppermute | solution.py:29
  37.9 3.9 %collective-permute-start.2 = (bf16[4,12,2,16]{3,2,1,0:T(2,128)(2,1)S(1)}, bf16[4,12,2,16]{3,2,1,0:T(2,128)(2,1)S(1)}, u32[]{:S(2)}, u32[]{:S(2)}) collective-permute-start(bf16[4,12,2,16]{3,2,1,0:T(2,128)(2,1)S(1)} %get-tuple-element.81), channel_id=1, source_target_pairs={{0,1},{2,3},{4,5},{6,7},{8,9},{10,11},{12,13},{14,15},{16,17},{18,... | collective-permute-start | bytes 9224 | tf_op jit(solution)/shard_map/ppermute | solution.py:28
  39.8 6.4 %collective-permute-start.3 = (bf16[4,12,2,16]{3,2,1,0:T(2,128)(2,1)S(1)}, bf16[4,12,2,16]{3,2,1,0:T(2,128)(2,1)S(1)}, u32[]{:S(2)}, u32[]{:S(2)}) collective-permute-start(bf16[4,12,2,16]{3,2,1,0:T(2,128)(2,1)S(1)} %get-tuple-element.82), channel_id=1, source_target_pairs={{1,0},{3,2},{5,4},{7,6},{9,8},{11,10},{13,12},{15,14},{17,16},{19,... | collective-permute-start | bytes 9224 | tf_op jit(solution)/shard_map/ppermute | solution.py:29
  46.3 2.4 %collective-permute-start.4 = (bf16[4,12,12,16]{3,2,1,0:T(8,128)(2,1)S(1)}, bf16[4,12,12,16]{3,2,1,0:T(8,128)(2,1)S(1)}, u32[]{:S(2)}, u32[]{:S(2)}) collective-permute-start(bf16[4,12,12,16]{3,2,1,0:T(8,128)(2,1)S(1)} %pad_maximum_fusion.18), channel_id=1, source_target_pairs={{0,8},{8,16},{16,24},{1,9},{9,17},{17,25},{2,10},{10,18},{18,26},{... | collective-permute-start | bytes 55304 | tf_op jit(solution)/shard_map/ppermute | solution.py:37
  61.2 0.9 copy-start.11
  61.8 0.9 copy-start.12
  61.8 0.9 copy-start.22
  62.4 0.9 copy-start.14
  62.4 0.9 copy-start.21
  63.0 0.9 copy-start.13
  63.0 0.9 copy-start.20
  63.6 0.8 copy-start.19
  64.2 0.8 copy-start.18
  64.7 0.8 copy-start.17
  65.3 0.8 copy-start.16
  67.8 1.4 copy-start.24
  69.2 45.1 %copy-start.25 = (f32[512]{0:T(512)S(1)}, f32[512]{0:T(512)}, u32[]{:S(2)}) copy-start(f32[512]{0:T(512)} %param.19) | copy-start | bytes 6148
  69.2 45.1 %copy-start.26 = (f32[512]{0:T(512)S(1)}, f32[512]{0:T(512)}, u32[]{:S(2)}) copy-start(f32[512]{0:T(512)} %param.18) | copy-start | bytes 6148
  192.7 2.3 %copy-start.2 = (bf16[4,8,8,1536]{3,2,1,0:T(8,128)(2,1)S(1)}, bf16[4,8,8,1536]{3,2,1,0:T(8,128)(2,1)}, u32[]{:S(2)}) copy-start(bf16[4,8,8,1536]{3,2,1,0:T(8,128)(2,1)} %pad_maximum_fusion.1) | copy-start | bytes 2359300
  195.0 1.1 copy-start.6
  196.1 1.1 copy-start.9
  197.3 1.1 copy-start.8
  198.4 1.1 copy-start.7
  199.5 1.1 copy-start.5
  200.7 1.1 copy-start.4
  201.8 1.1 copy-start.3
  202.4 2.0 copy-start.1
  202.9 0.7 copy-start.27
Sparse Core Ops, SparseCore 0:
  8.9 174.3 all-gather.2
